TPU v7x, 256 devices: a whole 4x4x8 slice. The times are simulated.
256 devices in a mesh: row: 32 (over y, z), col: 8 (over x, core).
Axes of the slice: x: 4, y: 4, z: 8, core: 2. Of those that a mesh axis runs over, the one named last changes fastest.
Arguments:
- lower: float32 [6, 2048, 2048], P(None, 'row', 'col'), may hold values from -0.046875 to 0.046875
- dinv: float32 [4, 2048, 2048], P(None, 'row', 'col'), as said below
- kcols: float32 [4, 2048, 2048], P(None, 'row', 'col'), may hold values from -6 to 6
- prior: float32 [2048], P('col'), may hold values from 3 to 5
Outputs:
- solved_columns: float32 [4, 2048, 2048], P(None, 'row', 'col')
- variance: float32 [2048], P('col')
Inputs may be any that keep to these rules, and one draw needn't show every extreme that they name: Each block of dinv is lower triangular with a positive diagonal.
All inputs are finite; a program needn't handle non-finite values.
Results may differ from a plain program's by a relative error of at most 0.0001.
Values sent between devices are 32-bit elements; how exact they have to be, the bound alone decides.
A program may use at most 64 MiB of HBM per device.

v0:
```python
import jax
import jax.numpy as jnp
from jax import lax
from jax.sharding import PartitionSpec as P

OBS = 8192


def append_block(gathered, section):
    return jnp.dot(
        section, gathered, precision=lax.Precision.HIGHEST, preferred_element_type=jnp.float32
    )


def remove_block(gathered, running, section):
    return running - jnp.dot(
        section, gathered, precision=lax.Precision.HIGHEST, preferred_element_type=jnp.float32
    )


def body(lower, dinv, kcols, prior):
    segments = kcols.shape[0]
    breadth = kcols.shape[2]
    bounds = [(0, breadth)]
    pending = [
        [kcols[segment_now, :, bound_pair[0] : bound_pair[1]] for segment_now in range(segments)]
        for bound_pair in bounds
    ]
    spread = [[] for bound_pair in bounds]
    solved = [[] for bound_pair in bounds]
    for segment_now in range(segments):
        residual = pending[0][segment_now]
        for earlier in range(segment_now):
            residual = remove_block(
                spread[0][earlier],
                residual,
                lax.all_gather(
                    lower[segment_now * (segment_now - 1) // 2 + earlier], "col", axis=1, tiled=True
                ),
            )
        whole_residual = lax.all_gather(residual, "row", axis=0, tiled=True)
        answer = append_block(
            whole_residual, lax.all_gather(dinv[segment_now], "col", axis=1, tiled=True)
        )
        solved[0].append(answer)
        if segment_now + 1 < segments:
            whole_answer = lax.all_gather(answer, "row", axis=0, tiled=True)
            spread[0].append(whole_answer)
    columns = [solved[0][segment_now] for segment_now in range(segments)]
    solution = jnp.stack(columns)
    squares = jnp.sum(solution * solution, axis=(0, 1))
    totals = lax.psum(squares, "row")
    variance = prior - totals / OBS
    return (solution, variance)


def solution(mesh):
    in_specs = (P(None, "row", "col"), P(None, "row", "col"), P(None, "row", "col"), P("col"))
    out_specs = (P(None, "row", "col"), P("col"))
    return jax.shard_map(body, mesh=mesh, in_specs=in_specs, out_specs=out_specs, check_vma=False)
```

profile of v0, /device:TPU:4, one launch (start us, length us, event | category | flops | bytes accessed | tf_op | source)
XLA Modules:
  0.0 652.7 jit_solution(342715879217123548)
XLA Ops:
  7.2 1.5 slice.43
  8.8 1.0 fusion.21
  9.8 13.3 %all-gather = f32[1,64,2048]{2,1,0:T(8,128)S(1)} all-gather(f32[1,64,256]{2,1,0:T(8,128)S(1)} %get-tuple-element.12), channel_id=2, replica_groups=mesh['row'=32,'col'=8] {'col'}, dimensions={2}, use_global_device_ids=true | all-gather | bytes 589824 | tf_op jit(solution)/shard_map/all_gather | solution.py:43
  23.1 69.0 %all-gather.31.cloned.1.call-done = f32[1,2048,256]{2,1,0:T(8,128)} async-done(((f32[1,64,256]{2,1,0:T(8,128)}), f32[1,2048,256]{2,1,0:T(8,128)}) %all-gather.31.cloned.1.call-update) | async-done | bytes 2097168 | tf_op jit(solution)/shard_map/all_gather | solution.py:41
  92.1 3.4 fusion
  95.6 11.9 %all-gather.2 = f32[1,64,2048]{2,1,0:T(8,128)S(1)} all-gather(f32[1,64,256]{2,1,0:T(8,128)S(1)} %get-tuple-element.7), channel_id=4, replica_groups=mesh['row'=32,'col'=8] {'col'}, dimensions={2}, use_global_device_ids=true | all-gather | bytes 589824 | tf_op jit(solution)/shard_map/all_gather | solution.py:37
  107.5 63.3 %all-gather.19.cloned.1.call-done = f32[2048,256]{1,0:T(8,128)} async-done(((f32[64,256]{1,0:T(8,128)}), f32[2048,256]{1,0:T(8,128)}) %all-gather.19.cloned.1.call-update) | async-done | bytes 2097168 | tf_op jit(solution)/shard_map/all_gather | solution.py:47
  170.8 3.6 fusion.2
  174.4 11.9 %all-gather.3 = f32[1,64,2048]{2,1,0:T(8,128)S(1)} all-gather(f32[1,64,256]{2,1,0:T(8,128)S(1)} %get-tuple-element.11), channel_id=5, replica_groups=mesh['row'=32,'col'=8] {'col'}, dimensions={2}, use_global_device_ids=true | all-gather | bytes 589824 | tf_op jit(solution)/shard_map/all_gather | solution.py:43
  186.3 63.3 %all-gather.21.cloned.1.call-done = f32[2048,256]{1,0:T(8,128)} async-done(((f32[64,256]{1,0:T(8,128)}), f32[2048,256]{1,0:T(8,128)}) %all-gather.21.cloned.1.call-update) | async-done | bytes 2097168 | tf_op jit(solution)/shard_map/all_gather | solution.py:41
  249.6 3.5 fusion.16
  253.3 12.0 %all-gather.5 = f32[1,64,2048]{2,1,0:T(8,128)S(1)} all-gather(f32[1,64,256]{2,1,0:T(8,128)S(1)} %get-tuple-element.5), channel_id=7, replica_groups=mesh['row'=32,'col'=8] {'col'}, dimensions={2}, use_global_device_ids=true | all-gather | bytes 589824 | tf_op jit(solution)/shard_map/all_gather | solution.py:37
  265.3 13.1 %all-gather.4 = f32[1,64,2048]{2,1,0:T(8,128)S(1)} all-gather(f32[1,64,256]{2,1,0:T(8,128)S(1)} %get-tuple-element.6), channel_id=6, replica_groups=mesh['row'=32,'col'=8] {'col'}, dimensions={2}, use_global_device_ids=true | all-gather | bytes 589824 | tf_op jit(solution)/shard_map/all_gather | solution.py:37
  278.4 50.1 %all-gather.23.cloned.1.call-done = f32[2048,256]{1,0:T(8,128)} async-done(((f32[64,256]{1,0:T(8,128)}), f32[2048,256]{1,0:T(8,128)}) %all-gather.23.cloned.1.call-update) | async-done | bytes 2097168 | tf_op jit(solution)/shard_map/all_gather | solution.py:47
  328.5 2.9 convolution_bitcast_fusion.4
  331.4 2.8 fusion.4
  334.3 11.9 %all-gather.6 = f32[1,64,2048]{2,1,0:T(8,128)S(1)} all-gather(f32[1,64,256]{2,1,0:T(8,128)S(1)} %get-tuple-element.13), channel_id=8, replica_groups=mesh['row'=32,'col'=8] {'col'}, dimensions={2}, use_global_device_ids=true | all-gather | bytes 589824 | tf_op jit(solution)/shard_map/all_gather | solution.py:43
  346.2 63.3 %all-gather.25.cloned.1.call-done = f32[2048,256]{1,0:T(8,128)} async-done(((f32[64,256]{1,0:T(8,128)}), f32[2048,256]{1,0:T(8,128)}) %all-gather.25.cloned.1.call-update) | async-done | bytes 2097168 | tf_op jit(solution)/shard_map/all_gather | solution.py:41
  409.5 3.6 fusion.12
  413.2 11.9 %all-gather.9 = f32[1,64,2048]{2,1,0:T(8,128)S(1)} all-gather(f32[1,64,256]{2,1,0:T(8,128)S(1)} %get-tuple-element.8), channel_id=11, replica_groups=mesh['row'=32,'col'=8] {'col'}, dimensions={2}, use_global_device_ids=true | all-gather | bytes 589824 | tf_op jit(solution)/shard_map/all_gather | solution.py:37
  425.1 13.3 %all-gather.8 = f32[1,64,2048]{2,1,0:T(8,128)S(1)} all-gather(f32[1,64,256]{2,1,0:T(8,128)S(1)} %get-tuple-element.9), channel_id=10, replica_groups=mesh['row'=32,'col'=8] {'col'}, dimensions={2}, use_global_device_ids=true | all-gather | bytes 589824 | tf_op jit(solution)/shard_map/all_gather | solution.py:37
  438.4 13.1 %all-gather.7 = f32[1,64,2048]{2,1,0:T(8,128)S(1)} all-gather(f32[1,64,256]{2,1,0:T(8,128)S(1)} %get-tuple-element.4), channel_id=9, replica_groups=mesh['row'=32,'col'=8] {'col'}, dimensions={2}, use_global_device_ids=true | all-gather | bytes 589824 | tf_op jit(solution)/shard_map/all_gather | solution.py:37
  451.4 2.9 convolution_bitcast_fusion.2
  454.4 34.0 %all-gather.27.cloned.1.call-done = f32[2048,256]{1,0:T(8,128)} async-done(((f32[64,256]{1,0:T(8,128)}), f32[2048,256]{1,0:T(8,128)}) %all-gather.27.cloned.1.call-update) | async-done | bytes 2097168 | tf_op jit(solution)/shard_map/all_gather | solution.py:47
  488.4 2.9 convolution_bitcast_fusion.1
  491.3 2.8 fusion.7
  494.2 12.0 %all-gather.10 = f32[1,64,2048]{2,1,0:T(8,128)S(1)} all-gather(f32[1,64,256]{2,1,0:T(8,128)S(1)} %get-tuple-element.10), channel_id=12, replica_groups=mesh['row'=32,'col'=8] {'col'}, dimensions={2}, use_global_device_ids=true | all-gather | bytes 589824 | tf_op jit(solution)/shard_map/all_gather | solution.py:43
  506.2 63.3 %all-gather.29.cloned.1.call-done = f32[2048,256]{1,0:T(8,128)} async-done(((f32[64,256]{1,0:T(8,128)}), f32[2048,256]{1,0:T(8,128)}) %all-gather.29.cloned.1.call-update) | async-done | bytes 2097168 | tf_op jit(solution)/shard_map/all_gather | solution.py:41
  569.5 2.9 convolution_bitcast_fusion
  572.4 0.7 multiply_reduce_fusion
  573.1 72.1 %psum.7 = f32[256]{0:T(256)S(1)} all-reduce(f32[256]{0:T(256)S(1)} %get-tuple-element.2), channel_id=1, replica_groups=mesh['row'=32,'col'=8] {'row'}, use_global_device_ids=true, to_apply=%region_1.0 | all-reduce | flops 256 | bytes 2048 | tf_op jit(solution)/shard_map/psum | solution.py:52
  645.2 0.6 multiply_subtract_fusion
  (27 shorter events, 0.5 us)
Async XLA Ops:
  7.2 88.4 %copy-start.4 = (f32[6,64,256]{2,1,0:T(8,128)S(1)}, f32[6,64,256]{2,1,0:T(8,128)}, u32[]{:S(2)}) copy-start(f32[6,64,256]{2,1,0:T(8,128)} %param.4) | copy-start | bytes 1179652
  7.2 84.9 %all-gather.31.cloned.1.call-start = ((), (), s32[]{:S(2)}) async-start(), calls=%async_computation.6 | async-start | bytes 2162688 | tf_op jit(solution)/shard_map/all_gather | solution.py:41
  8.8 162.0 %all-gather.19.cloned.1.call-start = ((), (), s32[]{:S(2)}) async-start(), calls=%async_computation | async-start | bytes 2162688 | tf_op jit(solution)/shard_map/all_gather | solution.py:47
  95.5 154.2 %all-gather.21.cloned.1.call-start = ((), (), s32[]{:S(2)}) async-start(), calls=%async_computation.1 | async-start | bytes 2162688 | tf_op jit(solution)/shard_map/all_gather | solution.py:41
  174.3 154.1 %all-gather.23.cloned.1.call-start = ((), (), s32[]{:S(2)}) async-start(), calls=%async_computation.2 | async-start | bytes 2162688 | tf_op jit(solution)/shard_map/all_gather | solution.py:47
  253.2 78.2 %copy-start = (f32[2048,256]{1,0:T(8,128)S(1)}, f32[2048,256]{1,0:T(8,128)}, u32[]{:S(2)}) copy-start(f32[2048,256]{1,0:T(8,128)} %all-gather.19.cloned.1.call-done) | copy-start | bytes 6291460
  253.2 156.3 %all-gather.25.cloned.1.call-start = ((), (), s32[]{:S(2)}) async-start(), calls=%async_computation.3 | async-start | bytes 2162688 | tf_op jit(solution)/shard_map/all_gather | solution.py:41
  334.3 154.1 %all-gather.27.cloned.1.call-start = ((), (), s32[]{:S(2)}) async-start(), calls=%async_computation.4 | async-start | bytes 2162688 | tf_op jit(solution)/shard_map/all_gather | solution.py:47
  413.1 156.3 %all-gather.29.cloned.1.call-start = ((), (), s32[]{:S(2)}) async-start(), calls=%async_computation.5 | async-start | bytes 2162688 | tf_op jit(solution)/shard_map/all_gather | solution.py:41
  494.1 78.3 %copy-start.1 = (f32[64,256]{1,0:T(8,128)S(1)}, f32[64,256]{1,0:T(8,128)}, u32[]{:S(2)}) copy-start(f32[64,256]{1,0:T(8,128)} %fusion) | copy-start | bytes 196612
  494.1 78.3 %copy-start.2 = (f32[256,64]{0,1:T(8,128)S(1)}, f32[256,64]{0,1:T(8,128)}, u32[]{:S(2)}) copy-start(f32[256,64]{0,1:T(8,128)} %fusion.16) | copy-start | bytes 196612
  494.1 78.3 %copy-start.3 = (f32[256,64]{0,1:T(8,128)S(1)}, f32[256,64]{0,1:T(8,128)}, u32[]{:S(2)}) copy-start(f32[256,64]{0,1:T(8,128)} %fusion.12) | copy-start | bytes 196612
  494.1 151.1 %copy-start.5 = (f32[256]{0:T(256)S(1)}, f32[256]{0:T(256)}, u32[]{:S(2)}) copy-start(f32[256]{0:T(256)} %param.7) | copy-start | bytes 3076
Sparse Core Ops, SparseCore 0:
  11.2 80.8 all-gather.30
  95.6 75.1 all-gather.18
  174.5 75.1 all-gather.20
  253.3 75.0 all-gather.22
  334.4 75.1 all-gather.24
  413.3 75.0 all-gather.26
  494.3 75.1 all-gather.28
where the time goes:
time: 653 us
  waiting for transfers between devices  406 us (62%)
  blocking collectives  197 us (30%)
  matrix products  31.4 us (5%)
  between operations  14.2 us (2%)
    all_gather x4, waiting for transfers between devices, body(): whole_residual = lax.all_gather(residual, 'row', axis=0, tiled=True)  259 us
    all_gather x3, waiting for transfers between devices, body(): whole_answer = lax.all_gather(answer, 'row', axis=0, tiled=True)  147 us
    all_gather x6, blocking collectives, body(): lax.all_gather(lower[segment_now * (segment_now - 1) // 2 + earlier], 'co...  75.3 us
    psum x1, blocking collectives, body(): totals = lax.psum(squares, 'row')  72.1 us
    all_gather x4, blocking collectives, body(): lax.all_gather(dinv[segment_now], 'col', axis=1, tiled=True)  49.1 us
    dot_general x6, matrix products, remove_block(): jnp.dot(section, gathered, precision=lax.Precision.HIGHEST, preferred_ele...  17.9 us
    dot_general x4, matrix products, append_block(): jnp.dot(section, gathered, precision=lax.Precision.HIGHEST, preferred_ele...  13.4 us
  transfers between devices with their start and end apart: 7, of which 7 were waited for; matrix products, arithmetic and copies ran while one was open for 1% of the time, Pallas kernels for 0%

commit v1 on v0

v1 whole, which is shorter than its diff:
```python
import functools

import jax
import jax.numpy as jnp
from jax import lax
from jax.experimental import pallas as pl
from jax.experimental.pallas import tpu as pltpu
from jax.sharding import PartitionSpec as P

OBS = 8192
MESH = pl.DeviceIdType.MESH
F32 = jnp.float32
BF16 = jnp.bfloat16


GROUPS = ((6, 1), (0, 1), (7, 1), (1, 2), (8, 1), (3, 3), (9, 1))


def kernel(
    X,
    lower_ref,
    dinv_ref,
    kcols_ref,
    prior_ref,
    out_ref,
    var_ref,
    G,
    HL,
    W,
    KB,
    XG,
    PB,
    RR,
    PE,
    VB,
    VX,
    VN,
    ring_s,
    ring_r,
    sib_s,
    sib_r,
    own_r,
    swap_s,
    gat_s,
    gat_r,
    red_s,
    red_r,
    k_s,
    k_r,
    out_s,
    out_r,
    vx_s,
    vx_r,
    vn_s,
    vn_r,
):
    Y, Z = X, 2 * X
    H = Z // 2
    row, col = lax.axis_index("row"), lax.axis_index("col")
    y, z = row // Z, lax.rem(row, Z)
    x, k = col // 2, lax.rem(col, 2)
    h = kcols_ref.shape[1]
    q = 2 * h
    w = kcols_ref.shape[2] // 2

    def dev(dx, dy, dz, dk):
        return (dy * Z + dz, dx * 2 + dk)

    def up(v, d, m):
        return lax.rem(v + d, m)

    pending = []

    class Copy:
        def __init__(self, src, dst, ssem, rsem, target, me=None):
            self.me = me
            self.remote = pltpu.make_async_remote_copy(
                src_ref=src, dst_ref=dst, send_sem=ssem, recv_sem=rsem, device_id=target, device_id_type=MESH
            )
            self.local = None if me is None else pltpu.make_async_copy(src, dst, rsem)

        def start(self):
            pending.append(self)
            if self.me is None:
                self.remote.start()
            else:
                pl.when(self.me)(self.local.start)
                pl.when(jnp.logical_not(self.me))(self.remote.start)

        def wait_send(self):
            if self.me is None:
                self.remote.wait_send()
            else:
                pl.when(jnp.logical_not(self.me))(self.remote.wait_send)

    def arrived(dst, rsem):
        pltpu.make_async_copy(dst, dst, rsem).wait()

    zu, zd = up(z, 1, Z), up(z, Z - 1, Z)
    above, below = dev(x, y, zu, k), dev(x, y, zd, k)
    sibling = dev(x, y, z, 1 - k)
    partner = dev(y, x, z, k)
    swaps_self = x == y
    xpeer = [None] + [dev(up(x, d, X), y, z, k) for d in range(1, X)]
    ypeer = [None] + [dev(x, up(y, d, Y), z, k) for d in range(1, Y)]
    k_to = [dev(y, z // 2, 2 * x + k, c) for c in range(2)]
    k_to_self = [(x == y) & (y == z // 2) & (z == 2 * x + k) & (k == c) for c in range(2)]
    k_from = [dev(z // 2, x, 2 * y + b, lax.rem(z, 2)) for b in range(2)]
    k_from_self = [(x == z // 2) & (y == x) & (z == 2 * y + b) & (k == lax.rem(z, 2)) for b in range(2)]
    o_to = [[dev(z // 2, yy, 2 * x + b, lax.rem(z, 2)) for b in range(2)] for yy in range(Y)]
    o_to_self = [
        [(x == z // 2) & (y == yy) & (z == 2 * x + b) & (k == lax.rem(z, 2)) for b in range(2)] for yy in range(Y)
    ]
    o_from = [[dev(z // 2, yy, 2 * x + k, c) for c in range(2)] for yy in range(Y)]
    o_from_self = [[(x == z // 2) & (y == yy) & (z == 2 * x + k) & (k == c) for c in range(2)] for yy in range(Y)]

    barrier = pltpu.get_barrier_semaphore()

    def greet(target, me=None):
        def far():
            pl.semaphore_signal(barrier, inc=1, device_id=target, device_id_type=MESH)

        if me is None:
            far()
        else:
            pl.when(jnp.logical_not(me))(far)

    for b in range(2):
        greet(k_from[b], k_from_self[b])
    for yy in range(Y):
        for c in range(2):
            greet(o_from[yy][c], o_from_self[yy][c])
    greet(partner, swaps_self)
    for d in range(1, X):
        greet(xpeer[d])
        greet(ypeer[d])
    greet(above)
    greet(below)
    greet(sibling)
    count = 2 * X + 1
    for me in k_to_self + [swaps_self] + [v for pair in o_to_self for v in pair]:
        count = count + jnp.where(me, 0, 1)
    own = pltpu.make_async_copy(dinv_ref, G.at[pl.ds(6, 4), k, z], own_r.at[0])
    own.start()
    pl.semaphore_wait(barrier, count)

    def piece(g, zz, kk):
        b0, nb = GROUPS[g]
        return G.at[pl.ds(b0, nb), kk, zz]

    def steps(g):
        return (H, Z - 1 - H) if g % 2 == 0 else (Z - 1 - H, H)

    def ring_send(g, upward, j):
        at = up(z, Z - j + 1, Z) if upward else up(z, j - 1, Z)
        lane = 0 if upward else 1
        Copy(
            piece(g, at, k),
            piece(g, at, k),
            ring_s.at[g, lane, j],
            ring_r.at[g, lane, j],
            above if upward else below,
        ).start()

    def sib_send(g, lane, j):
        at = up(z, Z - j, Z) if lane == 0 else up(z, j, Z)
        Copy(piece(g, at, k), piece(g, at, k), sib_s.at[g, lane, j], sib_r.at[g, lane, j], sibling).start()

    def relay(g, j):
        cu, cd = steps(g)
        if j == 1:
            if g % 2 == 1:
                arrived(piece(g, z, k), own_r.at[1 + g // 2])
            ring_send(g, True, 1)
            ring_send(g, False, 1)
            sib_send(g, 0, 0)
            return
        for lane, limit in ((0, cu), (1, cd)):
            if j - 1 <= limit:
                at = up(z, Z - j + 1, Z) if lane == 0 else up(z, j - 1, Z)
                arrived(piece(g, at, k), ring_r.at[g, lane, j - 1])
                if j <= limit:
                    ring_send(g, lane == 0, j)
                sib_send(g, lane, j - 1)

    def split(b):
        for kk in range(2):
            for j in range(X):
                block = jnp.concatenate([G[b, kk, 2 * j], G[b, kk, 2 * j + 1]], axis=0)
                hi = block.astype(BF16)
                HL[b, kk, j, pl.ds(0, q)] = hi
                HL[b, kk, j, pl.ds(q, q)] = (block - hi.astype(F32)).astype(BF16)

    def finish(g):
        cu, cd = steps(g)
        arrived(piece(g, z, 1 - k), sib_r.at[g, 0, 0])
        for lane, limit in ((0, cu), (1, cd)):
            for j in range(1, limit + 1):
                at = up(z, Z - j, Z) if lane == 0 else up(z, j, Z)
                arrived(piece(g, at, 1 - k), sib_r.at[g, lane, j])
        b0, nb = GROUPS[g]
        for b in range(b0, b0 + nb):
            split(b)

    own.wait()
    relay(0, 1)
    for part, (s0, ns) in enumerate(((0, 1), (1, 3))):
        for c in range(2):
            Copy(
                kcols_ref.at[pl.ds(s0, ns), :, pl.ds(c * w, w)],
                KB.at[pl.ds(s0, ns), lax.rem(z, 2)],
                k_s.at[part, c],
                k_r.at[part, lax.rem(z, 2)],
                k_to[c],
                k_to_self[c],
            ).start()
        if part == 0:
            for i, g in enumerate((1, 3, 5)):
                b0, nb = GROUPS[g]
                Copy(
                    lower_ref.at[pl.ds(b0, nb)],
                    piece(g, z, k),
                    swap_s.at[i],
                    own_r.at[1 + i],
                    partner,
                    swaps_self,
                ).start()

    def gather_start(i):
        n_at, peers = (y, ypeer) if i % 2 == 0 else (x, xpeer)
        for d in (2, 1, 3) if X == 4 else range(1, X):
            Copy(XG.at[i, n_at], XG.at[i, n_at], gat_s.at[i, d], gat_r.at[i, d], peers[d]).start()

    def gather_wait(i):
        n_at = y if i % 2 == 0 else x
        for d in range(1, X):
            arrived(XG.at[i, up(n_at, X - d, X)], gat_r.at[i, d])
        full = jnp.concatenate([XG[i, p] for p in range(X)], axis=0)
        hi = full.astype(BF16)
        lo = (full - hi.astype(F32)).astype(BF16)
        both = jnp.concatenate([hi, lo], axis=1)
        half = both.shape[0] // 2
        W[i, 0] = both[:half]
        W[i, 1] = both[half:]

    def product(i, b, j):
        res = jnp.dot(HL[b, 0, j], W[i, 0], preferred_element_type=F32)
        res += jnp.dot(HL[b, 1, j], W[i, 1], preferred_element_type=F32)
        return (res[:q, :w] + res[q:, w:]) + (res[:q, w:] + res[q:, :w])

    def reduce_start(i, blocks, early=None):
        n_at, peers = (x, xpeer) if i % 2 == 0 else (y, ypeer)
        for d in (2, 1, 3, 0) if X == 4 else list(range(1, X)) + [0]:
            j = up(n_at, d, X)
            total = None if early is None else PE[early, j]
            for src, b in blocks:
                term = product(src, b, j)
                total = term if total is None else total + term
            PB[i, d] = total
            if d:
                Copy(PB.at[i, d], RR.at[i, d], red_s.at[i, d], red_r.at[i, d], peers[d]).start()

    def early(slot, blocks):
        for j in range(X):
            total = None
            for src, b in blocks:
                term = product(src, b, j)
                total = term if total is None else total + term
            PE[slot, j] = total

    def reduce_wait(i):
        total = PB[i, 0]
        for d in range(1, X):
            arrived(RR.at[i, d], red_r.at[i, d])
            total = total + RR[i, d]
        return total

    def emit(s, solved, squares):
        src = XG.at[2 * s + 1, x] if s < 3 else PB.at[6, 0]
        for b in range(2):
            me = (x == z // 2) & (z == 2 * x + b) & (k == lax.rem(z, 2))
            Copy(
                src.at[pl.ds(b * h, h)],
                out_ref.at[s, :, pl.ds(pl.multiple_of(k * w, w), w)],
                out_s.at[s, b],
                out_r.at[s, k],
                dev(z // 2, y, 2 * x + b, lax.rem(z, 2)),
                me,
            ).start()
        part = jnp.sum(solved * solved, axis=0, keepdims=True)
        return part if squares is None else squares + part

    def step_in(s):
        if s:
            if s == 1:
                for b in range(2):
                    arrived(KB.at[pl.ds(1, 3), b], k_r.at[1, b])
            total = reduce_wait(2 * s - 1)
            XG[2 * s, y] = jnp.concatenate([KB[s, 0], KB[s, 1]], axis=0) - total
        else:
            for b in range(2):
                arrived(KB.at[pl.ds(0, 1), b], k_r.at[0, b])
            XG[0, y] = jnp.concatenate([KB[0, 0], KB[0, 1]], axis=0)
        gather_start(2 * s)

    last = H + 1
    relay(0, 2)
    relay(1, 1)
    step_in(0)
    for j in range(3, last + 1):
        relay(0, j)
        relay(1, j - 1)
        if j == 3:
            relay(2, 1)
        else:
            relay(2, j - 2)
    finish(0)
    gather_wait(0)
    reduce_start(0, [(0, 6)])
    relay(1, last)
    relay(2, last - 1)
    relay(3, 1)

    squares = None
    for s in range(3):
        solved = reduce_wait(2 * s)
        XG[2 * s + 1, x] = solved
        gather_start(2 * s + 1)
        squares = emit(s, solved, squares)
        if s == 0:
            relay(2, last)
            relay(3, 2)
            finish(1)
            gather_wait(1)
            reduce_start(1, [(1, 0)])
            relay(3, 3)
            relay(4, 1)
        elif s == 1:
            relay(4, 4)
            relay(5, 3)
            relay(6, 1)
            gather_wait(3)
            reduce_start(3, [(3, 2)], early=0)
            relay(4, 5)
            relay(5, 4)
            relay(6, 2)
            finish(4)
        else:
            relay(6, 5)
            gather_wait(5)
            reduce_start(5, [(5, 5)], early=1)
            finish(6)
        step_in(s + 1)
        if s == 0:
            relay(3, 4)
            relay(4, 2)
            relay(5, 1)
            finish(2)
            gather_wait(2)
            reduce_start(2, [(2, 7)])
            relay(3, 5)
            relay(4, 3)
            relay(5, 2)
            finish(3)
            early(0, [(1, 1)])
        elif s == 1:
            relay(5, 5)
            relay(6, 3)
            gather_wait(4)
            reduce_start(4, [(4, 8)])
            relay(6, 4)
            finish(5)
            early(1, [(1, 3), (3, 4)])
        else:
            gather_wait(6)
            reduce_start(6, [(6, 9)])
    solved = reduce_wait(6)
    PB[6, 0] = solved
    squares = emit(3, solved, squares)

    VB[0] = jnp.broadcast_to(squares, VB.shape[1:])
    for d in range(1, X):
        Copy(VB.at[0], VX.at[d], vx_s.at[d], vx_r.at[d], xpeer[d]).start()
    total = VB[0]
    for d in range(1, X):
        arrived(VX.at[d], vx_r.at[d])
        total = total + VX[d]
    VB[1] = total
    for yy in range(Y):
        for b in range(2):
            Copy(
                VB.at[1], VN.at[y, k], vn_s.at[yy, b], vn_r.at[y, k], o_to[yy][b], o_to_self[yy][b]
            ).start()
    for yy in range(Y):
        for c in range(2):
            arrived(VN.at[yy, c], vn_r.at[yy, c])
    for c in range(2):
        total = VN[0, c]
        for yy in range(1, Y):
            total = total + VN[yy, c]
        var_ref[:, pl.ds(c * w, w)] = prior_ref[:, pl.ds(c * w, w)] - total[0:1] / OBS
    for s in range(4):
        for c in range(2):
            arrived(out_ref.at[s, :, pl.ds(c * w, w)], out_r.at[s, c])
    for copy in pending:
        copy.wait_send()


def body(X, lower, dinv, kcols, prior):
    h, wide = kcols.shape[1], kcols.shape[2]
    q, w, Z = 2 * h, wide // 2, 2 * X
    vmem = pl.BlockSpec(memory_space=pltpu.VMEM)
    dma = pltpu.SemaphoreType.DMA
    out, var = pl.pallas_call(
        functools.partial(kernel, X),
        out_shape=(
            jax.ShapeDtypeStruct(kcols.shape, F32),
            jax.ShapeDtypeStruct((1, wide), F32),
        ),
        in_specs=[vmem] * 4,
        out_specs=(vmem, vmem),
        scratch_shapes=[
            pltpu.VMEM((10, 2, Z, h, wide), F32),
            pltpu.VMEM((10, 2, X, 2 * q, wide), BF16),
            pltpu.VMEM((7, 2, X * q // 2, 2 * w), BF16),
            pltpu.VMEM((4, 2, h, w), F32),
            pltpu.VMEM((7, X, q, w), F32),
            pltpu.VMEM((7, X, q, w), F32),
            pltpu.VMEM((7, X, q, w), F32),
            pltpu.VMEM((2, X, q, w), F32),
            pltpu.VMEM((2, 8, w), F32),
            pltpu.VMEM((X, 8, w), F32),
            pltpu.VMEM((X, 2, 8, w), F32),
            dma((7, 2, Z // 2 + 1)),
            dma((7, 2, Z // 2 + 1)),
            dma((7, 2, Z // 2 + 1)),
            dma((7, 2, Z // 2 + 1)),
            dma((4,)),
            dma((3,)),
            dma((7, X)),
            dma((7, X)),
            dma((7, X)),
            dma((7, X)),
            dma((2, 2)),
            dma((2, 2)),
            dma((4, 2)),
            dma((4, 2)),
            dma((X,)),
            dma((X,)),
            dma((X, 2)),
            dma((X, 2)),
        ],
        compiler_params=pltpu.CompilerParams(
            collective_id=0, has_side_effects=True, vmem_limit_bytes=60 * 1024 * 1024
        ),
    )(lower, dinv, kcols, prior.reshape(1, wide))
    return out, var.reshape(wide)


def solution(mesh):
    in_specs = (P(None, "row", "col"), P(None, "row", "col"), P(None, "row", "col"), P("col"))
    out_specs = (P(None, "row", "col"), P("col"))
    return jax.shard_map(
        functools.partial(body, mesh.shape["col"] // 2),
        mesh=mesh,
        in_specs=in_specs,
        out_specs=out_specs,
        check_vma=False,
    )
```

time: 653 us -> 151 us (0.23)
  waiting for transfers between devices: 406 us -> 0 us
  blocking collectives: 197 us -> 0 us
  Pallas kernels: 0 us -> 147 us
  matrix products: 31.4 us -> 0 us
  between operations: 14.2 us -> 0.65 us
    all_gather x7 -> x0, waiting for transfers between devices: 406 us -> none  [the longest x4 259 us: body(): whole_residual = lax.all_gather(residual, 'row', axis=0, tiled=True)]
    pallas_call x0 -> x1, Pallas kernels: none -> 147 us  [body(): pl.pallas_call(functools.partial(kernel, X), out_shape=(jax.ShapeDtypeStr...]
    all_gather x10 -> x0, blocking collectives: 124 us -> none  [the longest x6 75.3 us: body(): lax.all_gather(lower[segment_now * (segment_now - 1) // 2 + earlier], 'co...]
    psum x1 -> x0, blocking collectives: 72.1 us -> none  [body(): totals = lax.psum(squares, 'row')]
    dot_general x10 -> x0, matrix products: 31.4 us -> none  [the longest x6 17.9 us: remove_block(): jnp.dot(section, gathered, precision=lax.Precision.HIGHEST, preferred_ele...]
  transfers between devices with their start and end apart: 7 -> 0, of which waited for: 7 -> 0; matrix products, arithmetic and copies ran while one was open for 1% -> 0% of each run, Pallas kernels for 0% -> 0%
where the time goes in v1:
time: 151 us; the launch traced here: 150 us
  Pallas kernels  147 us (97%)
  local copies, waits for them, and re-layouts  2.24 us (1%)
    pallas_call x1, Pallas kernels, body(): pl.pallas_call(functools.partial(kernel, X), out_shape=(jax.ShapeDtypeStr...  147 us

profile of v1, /device:TPU:4, one launch (start us, length us, event | category | flops | bytes accessed | tf_op | source)
XLA Modules:
  0.0 149.9 jit_solution(1364544440448928686)
XLA Ops:
  0.6 147.0 %shard_map.59 = (f32[4,64,256]{2,1,0:T(8,128)}, f32[1,256]{1,0:T(1,128)}) custom-call(f32[6,64,256]{2,1,0:T(8,128)} %lower_ref.1, f32[4,64,256]{2,1,0:T(8,128)} %dinv_ref.1, f32[4,64,256]{2,1,0:T(8,128)} %kcols_ref.1, f32[1,256]{1,0:T(1,128)} %bitcast.3), custom_call_target="tpu_custom_call" | custom-call | tf_op jit(solution)/shard_map/pallas_call | solution.py:414
  147.7 0.0 copy-start
  147.7 1.7 %copy.8 = f32[4,64,256]{2,1,0:T(8,128)} copy(f32[4,64,256]{2,1,0:T(8,128)} %get-tuple-element.8) | data formatting | bytes 524288
  149.4 0.0 copy-done
  149.4 0.6 copy.9
Async XLA Ops:
  147.7 1.7 %copy-start = (f32[1,256]{1,0:T(1,128)S(1)}, f32[1,256]{1,0:T(1,128)}, u32[]{:S(2)}) copy-start(f32[1,256]{1,0:T(1,128)} %get-tuple-element.5) | copy-start | bytes 3076

commit v2 on v1

v2 whole, which is shorter than its diff:
```python
import functools

import jax
import jax.numpy as jnp
from jax import lax
from jax.experimental import pallas as pl
from jax.experimental.pallas import tpu as pltpu
from jax.sharding import PartitionSpec as P

OBS = 8192
MESH = pl.DeviceIdType.MESH
F32 = jnp.float32
BF16 = jnp.bfloat16


ORDER = (6, 0, 7, 1, 2, 8, 3, 4, 5, 9)
GROUPS = tuple((b, 1) for b in ORDER)


def kernel(
    X,
    lower_ref,
    dinv_ref,
    kcols_ref,
    prior_ref,
    out_ref,
    var_ref,
    G,
    HL,
    W,
    KX,
    KB,
    XG,
    PB,
    RR,
    PE,
    OB,
    VB,
    VP,
    VZ,
    ring_s,
    ring_r,
    sib_s,
    sib_r,
    own_s,
    own_r,
    gat_s,
    gat_r,
    red_s,
    red_r,
    kx_s,
    kx_r,
    kz_s,
    kz_r,
    oz_s,
    oz_r,
    ox_s,
    ox_r,
    vp_s,
    vp_r,
    vz_s,
    vz_r,
):
    Y, Z = X, 2 * X
    H = Z // 2
    row, col = lax.axis_index("row"), lax.axis_index("col")
    y, z = row // Z, lax.rem(row, Z)
    x, k = col // 2, lax.rem(col, 2)
    h = kcols_ref.shape[1]
    t = h // X
    q = Z * t
    w = kcols_ref.shape[2] // 2

    def dev(dx, dy, dz, dk):
        return (dy * Z + dz, dx * 2 + dk)

    def up(v, d, m):
        return lax.rem(v + d, m)

    pending = []

    class Copy:
        def __init__(self, src, dst, ssem, rsem, target, me=None):
            self.me = me
            self.remote = pltpu.make_async_remote_copy(
                src_ref=src, dst_ref=dst, send_sem=ssem, recv_sem=rsem, device_id=target, device_id_type=MESH
            )
            self.local = None if me is None else pltpu.make_async_copy(src, dst, rsem)

        def start(self):
            pending.append(self)
            if self.me is None:
                self.remote.start()
            else:
                pl.when(self.me)(self.local.start)
                pl.when(jnp.logical_not(self.me))(self.remote.start)

        def wait_send(self):
            if self.me is None:
                self.remote.wait_send()
            else:
                pl.when(jnp.logical_not(self.me))(self.remote.wait_send)

    def arrived(dst, rsem):
        pltpu.make_async_copy(dst, dst, rsem).wait()

    xpeer = [None] + [dev(up(x, d, X), y, z, k) for d in range(1, X)]
    ypeer = [None] + [dev(x, up(y, d, Y), z, k) for d in range(1, Y)]
    zpeer = [None] + [dev(x, y, up(z, d, Z), k) for d in range(1, Z)]
    sibling = dev(x, y, z, 1 - k)
    far = (2, 1, 3) if X == 4 else tuple(range(1, X))

    barrier = pltpu.get_barrier_semaphore()

    def greet(target, me=None):
        def signal():
            pl.semaphore_signal(barrier, inc=1, device_id=target, device_id_type=MESH)

        if me is None:
            signal()
        else:
            pl.when(jnp.logical_not(me))(signal)

    mine = x == z // 2
    for target in zpeer[1:] + xpeer[1:] + ypeer[1:] + [sibling]:
        greet(target)
    for yy in range(Y):
        greet(dev(y, yy, z, k), (x == y) & (y == yy))
    for xx in range(X):
        for yy in range(Y):
            pl.when(mine)(functools.partial(greet, dev(xx, yy, z, k), (x == xx) & (y == yy)))
    pl.semaphore_wait(barrier, 2 * Z + 2 * X - 2 + X + Y - Z - jnp.where(x == y, 1, 0) - jnp.where(mine, 1, 0))

    def piece(g, zz, kk):
        b0, nb = GROUPS[g]
        return G.at[pl.ds(b0, nb), kk, zz]

    def spread(g):
        b0, nb = GROUPS[g]
        src = lower_ref.at[pl.ds(b0, nb)] if b0 < 6 else dinv_ref.at[pl.ds(b0 - 6, nb)]
        for xx in range(X):
            Copy(
                src.at[:, pl.ds(xx * t, t), :],
                G.at[pl.ds(b0, nb), k, z, y],
                own_s.at[g, xx],
                own_r.at[g, y],
                dev(xx, x, z, k),
                (x == xx) & (x == y),
            ).start()

    def z_send(g, d, what, lane, rows=None):
        at = up(z, what % Z, Z)
        ref = piece(g, at, k)
        if rows is not None:
            ref = ref.at[:, pl.ds(*rows)]
        Copy(ref, ref, ring_s.at[g, lane], ring_r.at[g, lane], zpeer[d % Z]).start()

    def z_arrived(g, what, lane, rows=None):
        ref = piece(g, up(z, what % Z, Z), k)
        if rows is not None:
            ref = ref.at[:, pl.ds(*rows)]
        arrived(ref, ring_r.at[g, lane])

    def sib_send(g, what):
        ref = piece(g, up(z, what % Z, Z), k)
        Copy(ref, ref, sib_s.at[g, what % Z], sib_r.at[g, what % Z], sibling).start()

    lower_half, upper_half = (0, Y // 2), (Y // 2, Y - Y // 2)

    def relay(g, j):
        if j == 1:
            b0, nb = GROUPS[g]
            for yy in range(Y):
                arrived(G.at[pl.ds(b0, nb), k, z, yy], own_r.at[g, yy])
            z_send(g, 1, 0, 0)
            z_send(g, -1, 0, 1)
            sib_send(g, 0)
        elif j <= H:
            for sign in (1, -1):
                what, lane = -sign * (j - 1), 2 * (j - 2) + (0 if sign == 1 else 1)
                z_arrived(g, what, lane)
                rows = None if j < H else (lower_half if sign == 1 else upper_half)
                z_send(g, sign, what, lane + 2, rows)
                sib_send(g, what)
        else:
            z_arrived(g, H, 2 * H - 2, lower_half)
            z_arrived(g, H, 2 * H - 1, upper_half)
            sib_send(g, H)

    STARTS = (0, 1, 3, 5, 6, 7, 8, 9, 10, 11)

    def slot(n):
        for g, first in enumerate(STARTS):
            if 1 <= n - first + 1 <= H + 1:
                relay(g, n - first + 1)

    def split(b):
        for kk in range(2):
            for j in range(Y):
                block = G[b, kk, :, j].reshape(q, 2 * w)
                hi = block.astype(BF16)
                HL[b, kk, j, pl.ds(0, q)] = hi
                HL[b, kk, j, pl.ds(q, q)] = (block - hi.astype(F32)).astype(BF16)

    def finish(g):
        for zz in range(Z):
            arrived(piece(g, up(z, zz, Z), 1 - k), sib_r.at[g, zz])
        b0, nb = GROUPS[g]
        for b in range(b0, b0 + nb):
            split(b)

    PARTS = ((0, 1), (1, 3))

    def strip(xx):
        return pl.ds(pl.multiple_of(xx * t, t), t)

    def half(zz):
        return pl.ds(pl.multiple_of(lax.rem(zz, 2) * w, w), w)

    def columns(part):
        ss = pl.ds(*PARTS[part])
        for d in far:
            Copy(
                kcols_ref.at[ss, strip(up(x, d, X))], KX.at[ss, x], kx_s.at[part, d], kx_r.at[part, d], xpeer[d]
            ).start()
        pltpu.make_async_copy(kcols_ref.at[ss, strip(x)], KX.at[ss, x], kx_r.at[part, 0]).start()

    def columns_on(part):
        ss = pl.ds(*PARTS[part])
        for d in range(X):
            arrived(KX.at[ss, up(x, X - d, X)], kx_r.at[part, d])
        for d in (4, 3, 5, 2, 6, 1, 7) if Z == 8 else range(1, Z):
            zz = up(z, d, Z)
            Copy(
                KX.at[ss, zz // 2, :, half(zz)], KB.at[ss, z], kz_s.at[part, d], kz_r.at[part, d], zpeer[d]
            ).start()
        pltpu.make_async_copy(KX.at[ss, z // 2, :, half(z)], KB.at[ss, z], kz_r.at[part, 0]).start()

    def columns_wait(part):
        ss = pl.ds(*PARTS[part])
        for d in range(Z):
            arrived(KB.at[ss, up(z, Z - d, Z)], kz_r.at[part, d])

    def gather_start(i):
        for d in far:
            Copy(XG.at[i, :, x], XG.at[i, :, x], gat_s.at[i, d], gat_r.at[i, d], xpeer[d]).start()

    def gather_wait(i):
        for d in range(1, X):
            arrived(XG.at[i, :, up(x, X - d, X)], gat_r.at[i, d])
        full = XG[i].reshape(X * q, w)
        hi = full.astype(BF16)
        lo = (full - hi.astype(F32)).astype(BF16)
        both = jnp.concatenate([hi, lo], axis=1)
        half = both.shape[0] // 2
        W[i, 0] = both[:half]
        W[i, 1] = both[half:]

    def product(i, b, j):
        res = jnp.dot(HL[b, 0, j], W[i, 0], preferred_element_type=F32)
        res += jnp.dot(HL[b, 1, j], W[i, 1], preferred_element_type=F32)
        return (res[:q, :w] + res[q:, w:]) + (res[:q, w:] + res[q:, :w])

    def reduce_start(i, blocks, early=None):
        for d in far + (0,):
            j = up(y, d, Y)
            total = None if early is None else PE[early, j]
            for src, b in blocks:
                term = product(src, b, j)
                total = term if total is None else total + term
            PB[i, d] = total
            if d:
                Copy(PB.at[i, d], RR.at[i, d], red_s.at[i, d], red_r.at[i, d], ypeer[d]).start()

    def early(slot, blocks):
        for j in range(Y):
            total = None
            for src, b in blocks:
                term = product(src, b, j)
                total = term if total is None else total + term
            PE[slot, j] = total

    def reduce_wait(i):
        total = PB[i, 0]
        for d in range(1, Y):
            arrived(RR.at[i, d], red_r.at[i, d])
            total = total + RR[i, d]
        return total

    def emit(s, solved, squares):
        src = XG.at[2 * s + 1]
        for d in (4, 3, 5, 2, 6, 1, 7) if Z == 8 else range(1, Z):
            Copy(
                src.at[up(z, d, Z), x], OB.at[s, z // 2, :, half(z)], oz_s.at[s, d], oz_r.at[s, d], zpeer[d]
            ).start()
        pltpu.make_async_copy(src.at[z, x], OB.at[s, z // 2, :, half(z)], oz_r.at[s, 0]).start()
        part = jnp.sum(solved * solved, axis=0, keepdims=True)
        return part if squares is None else squares + part

    def deliver(s):
        for d in range(Z):
            zz = up(z, Z - d, Z)
            arrived(OB.at[s, zz // 2, :, half(zz)], oz_r.at[s, d])
        for d in far:
            Copy(OB.at[s, up(x, d, X)], out_ref.at[s, strip(x)], ox_s.at[s, d], ox_r.at[s, d], xpeer[d]).start()
        pltpu.make_async_copy(OB.at[s, x], out_ref.at[s, strip(x)], ox_r.at[s, 0]).start()

    def step_in(s):
        columns = KB[s].reshape(q, w)
        if s:
            columns = columns - reduce_wait(2 * s - 1)
        XG[2 * s, :, x] = columns.reshape(Z, t, w)
        gather_start(2 * s)

    spread(0)
    columns(0)
    spread(1)
    spread(2)
    columns(1)
    for g in range(3, 10):
        spread(g)

    slot(0)
    columns_on(0)
    slot(1)
    slot(2)
    columns_wait(0)
    step_in(0)
    slot(3)
    columns_on(1)
    slot(4)
    finish(0)
    gather_wait(0)
    reduce_start(0, [(0, 6)])
    slot(5)

    squares = None
    for s in range(3):
        solved = reduce_wait(2 * s)
        XG[2 * s + 1, :, x] = solved.reshape(Z, t, w)
        gather_start(2 * s + 1)
        squares = emit(s, solved, squares)
        slot(4 * s + 6)
        if s == 0:
            finish(1)
            gather_wait(1)
            reduce_start(1, [(1, 0)])
            columns_wait(1)
        elif s == 1:
            finish(4)
            gather_wait(3)
            reduce_start(3, [(3, 2)], early=0)
        else:
            finish(7)
            early(1, [(1, 3), (3, 4)])
            finish(8)
            gather_wait(5)
            reduce_start(5, [(5, 5)], early=1)
        slot(4 * s + 7)
        deliver(s)
        step_in(s + 1)
        slot(4 * s + 8)
        if s == 0:
            finish(2)
            gather_wait(2)
            reduce_start(2, [(2, 7)])
        elif s == 1:
            finish(5)
            gather_wait(4)
            reduce_start(4, [(4, 8)])
        else:
            finish(9)
            gather_wait(6)
            reduce_start(6, [(6, 9)])
        slot(4 * s + 9)
        if s == 0:
            finish(3)
            early(0, [(1, 1)])
        elif s == 1:
            finish(6)
    solved = reduce_wait(6)
    XG[7, :, x] = solved.reshape(Z, t, w)
    squares = emit(3, solved, squares)

    VB[0] = jnp.broadcast_to(squares, VB.shape[1:])
    for yy in range(Y):
        Copy(
            VB.at[0], VP.at[x, y], vp_s.at[yy], vp_r.at[x, y], dev(z // 2, yy, z, k), mine & (y == yy)
        ).start()

    @pl.when(mine)
    def _():
        total = None
        for xx in range(X):
            for yy in range(Y):
                arrived(VP.at[xx, yy], vp_r.at[xx, yy])
                total = VP[xx, yy] if total is None else total + VP[xx, yy]
        VB[1] = total
        for d in range(1, Z):
            pltpu.make_async_remote_copy(
                src_ref=VB.at[1],
                dst_ref=VZ.at[lax.rem(z, 2)],
                send_sem=vz_s.at[d],
                recv_sem=vz_r.at[lax.rem(z, 2)],
                device_id=zpeer[d],
                device_id_type=MESH,
            ).start()
        pltpu.make_async_copy(VB.at[1], VZ.at[lax.rem(z, 2)], vz_r.at[lax.rem(z, 2)]).start()

    deliver(3)
    for c in range(2):
        arrived(VZ.at[c], vz_r.at[c])
        var_ref[:, pl.ds(c * w, w)] = prior_ref[:, pl.ds(c * w, w)] - VZ[c, 0:1] / OBS
    for s in range(4):
        for d in range(X):
            arrived(out_ref.at[s, strip(up(x, X - d, X))], ox_r.at[s, d])

    @pl.when(mine)
    def _():
        for d in range(1, Z):
            pltpu.make_async_remote_copy(
                src_ref=VB.at[1],
                dst_ref=VZ.at[lax.rem(z, 2)],
                send_sem=vz_s.at[d],
                recv_sem=vz_r.at[lax.rem(z, 2)],
                device_id=zpeer[d],
                device_id_type=MESH,
            ).wait_send()

    for copy in pending:
        copy.wait_send()


def body(X, lower, dinv, kcols, prior):
    h, wide = kcols.shape[1], kcols.shape[2]
    Z, t, w = 2 * X, h // X, wide // 2
    q = Z * t
    vmem = pl.BlockSpec(memory_space=pltpu.VMEM)
    dma = pltpu.SemaphoreType.DMA
    out, var = pl.pallas_call(
        functools.partial(kernel, X),
        out_shape=(
            jax.ShapeDtypeStruct(kcols.shape, F32),
            jax.ShapeDtypeStruct((1, wide), F32),
        ),
        in_specs=[vmem] * 4,
        out_specs=(vmem, vmem),
        scratch_shapes=[
            pltpu.VMEM((10, 2, Z, X, t, wide), F32),
            pltpu.VMEM((10, 2, X, 2 * q, wide), BF16),
            pltpu.VMEM((7, 2, X * q // 2, wide), BF16),
            pltpu.VMEM((4, X, t, wide), F32),
            pltpu.VMEM((4, Z, t, w), F32),
            pltpu.VMEM((8, Z, X, t, w), F32),
            pltpu.VMEM((7, X, q, w), F32),
            pltpu.VMEM((7, X, q, w), F32),
            pltpu.VMEM((2, X, q, w), F32),
            pltpu.VMEM((4, X, t, wide), F32),
            pltpu.VMEM((2, 8, w), F32),
            pltpu.VMEM((X, X, 8, w), F32),
            pltpu.VMEM((2, 8, w), F32),
            dma((10, 8)),
            dma((10, 8)),
            dma((10, Z)),
            dma((10, Z)),
            dma((10, X)),
            dma((10, X)),
            dma((7, X)),
            dma((7, X)),
            dma((7, X)),
            dma((7, X)),
            dma((2, X)),
            dma((2, X)),
            dma((2, Z)),
            dma((2, Z)),
            dma((4, Z)),
            dma((4, Z)),
            dma((4, X)),
            dma((4, X)),
            dma((X,)),
            dma((X, X)),
            dma((Z,)),
            dma((2,)),
        ],
        compiler_params=pltpu.CompilerParams(
            collective_id=0, has_side_effects=True, vmem_limit_bytes=60 * 1024 * 1024
        ),
    )(lower, dinv, kcols, prior.reshape(1, wide))
    return out, var.reshape(wide)


def solution(mesh):
    in_specs = (P(None, "row", "col"), P(None, "row", "col"), P(None, "row", "col"), P("col"))
    out_specs = (P(None, "row", "col"), P("col"))
    return jax.shard_map(
        functools.partial(body, mesh.shape["col"] // 2),
        mesh=mesh,
        in_specs=in_specs,
        out_specs=out_specs,
        check_vma=False,
    )
```

time: 151 us -> 118 us (0.78)
  Pallas kernels: 147 us -> 115 us
    pallas_call x1, Pallas kernels: 147 us -> 115 us  [body(): pl.pallas_call(functools.partial(kernel, X), out_shape=(jax.ShapeDtypeStr...]
where the time goes in v2:
time: 118 us
  Pallas kernels  115 us (97%)
  local copies, waits for them, and re-layouts  2.24 us (2%)
    pallas_call x1, Pallas kernels, body(): pl.pallas_call(functools.partial(kernel, X), out_shape=(jax.ShapeDtypeStr...  115 us

profile of v2, /device:TPU:4, one launch (start us, length us, event | category | flops | bytes accessed | tf_op | source)
XLA Modules:
  0.0 118.1 jit_solution(11619611063070928580)
XLA Ops:
  0.6 115.2 %shard_map.59 = (f32[4,64,256]{2,1,0:T(8,128)}, f32[1,256]{1,0:T(1,128)}) custom-call(f32[6,64,256]{2,1,0:T(8,128)} %lower_ref.1, f32[4,64,256]{2,1,0:T(8,128)} %dinv_ref.1, f32[4,64,256]{2,1,0:T(8,128)} %kcols_ref.1, f32[1,256]{1,0:T(1,128)} %bitcast.3), custom_call_target="tpu_custom_call" | custom-call | tf_op jit(solution)/shard_map/pallas_call | solution.py:440
  115.8 0.0 copy-start
  115.8 1.7 %copy.8 = f32[4,64,256]{2,1,0:T(8,128)} copy(f32[4,64,256]{2,1,0:T(8,128)} %get-tuple-element.8) | data formatting | bytes 524288
  117.5 0.0 copy-done
  117.5 0.6 copy.9
Async XLA Ops:
  115.8 1.7 %copy-start = (f32[1,256]{1,0:T(1,128)S(1)}, f32[1,256]{1,0:T(1,128)}, u32[]{:S(2)}) copy-start(f32[1,256]{1,0:T(1,128)} %get-tuple-element.5) | copy-start | bytes 3076

commit v3 on v2

--- a/solution.py
+++ b/solution.py
@@ -187,7 +187,7 @@
             z_arrived(g, H, 2 * H - 1, upper_half)
             sib_send(g, H)
 
-    STARTS = (0, 1, 3, 5, 6, 7, 8, 9, 10, 11)
+    STARTS = (0, 1, 3, 5, 6, 8, 9, 10, 10, 12)
 
     def slot(n):
         for g, first in enumerate(STARTS):
@@ -196,11 +196,12 @@
 
     def split(b):
         for kk in range(2):
-            for j in range(Y):
-                block = G[b, kk, :, j].reshape(q, 2 * w)
-                hi = block.astype(BF16)
-                HL[b, kk, j, pl.ds(0, q)] = hi
-                HL[b, kk, j, pl.ds(q, q)] = (block - hi.astype(F32)).astype(BF16)
+            for f in range(2):
+                for j in range(Y):
+                    block = G[b, kk, pl.ds(f * H, H), j].reshape(q // 2, 2 * w)
+                    hi = block.astype(BF16)
+                    HL[b, kk, f, j, pl.ds(0, q // 2)] = hi
+                    HL[b, kk, f, j, pl.ds(q // 2, q // 2)] = (block - hi.astype(F32)).astype(BF16)
 
     def finish(g):
         for zz in range(Z):
@@ -241,61 +242,60 @@
         for d in range(Z):
             arrived(KB.at[ss, up(z, Z - d, Z)], kz_r.at[part, d])
 
-    def gather_start(i):
+    def gather_start(i, f):
+        ref = XG.at[i, pl.ds(f * H, H), x]
         for d in far:
-            Copy(XG.at[i, :, x], XG.at[i, :, x], gat_s.at[i, d], gat_r.at[i, d], xpeer[d]).start()
+            Copy(ref, ref, gat_s.at[i, f, d], gat_r.at[i, f, d], xpeer[d]).start()
 
     def gather_wait(i):
-        for d in range(1, X):
-            arrived(XG.at[i, :, up(x, X - d, X)], gat_r.at[i, d])
-        full = XG[i].reshape(X * q, w)
-        hi = full.astype(BF16)
-        lo = (full - hi.astype(F32)).astype(BF16)
-        both = jnp.concatenate([hi, lo], axis=1)
-        half = both.shape[0] // 2
-        W[i, 0] = both[:half]
-        W[i, 1] = both[half:]
-
-    def product(i, b, j):
-        res = jnp.dot(HL[b, 0, j], W[i, 0], preferred_element_type=F32)
-        res += jnp.dot(HL[b, 1, j], W[i, 1], preferred_element_type=F32)
-        return (res[:q, :w] + res[q:, w:]) + (res[:q, w:] + res[q:, :w])
+        for f in range(2):
+            for d in range(1, X):
+                arrived(XG.at[i, pl.ds(f * H, H), up(x, X - d, X)], gat_r.at[i, f, d])
+            full = XG[i, pl.ds(f * H, H)].reshape(X * q // 2, w)
+            hi = full.astype(BF16)
+            lo = (full - hi.astype(F32)).astype(BF16)
+            W[i, f] = jnp.concatenate([hi, lo], axis=1)
+
+    def product(i, b, f, j):
+        p = q // 2
+        res = jnp.dot(HL[b, 0, f, j], W[i, 0], preferred_element_type=F32)
+        res += jnp.dot(HL[b, 1, f, j], W[i, 1], preferred_element_type=F32)
+        return (res[:p, :w] + res[p:, w:]) + (res[:p, w:] + res[p:, :w])
+
+    def products(blocks, f, j, total=None):
+        for src, b in blocks:
+            term = product(src, b, f, j)
+            total = term if total is None else total + term
+        return total
 
     def reduce_start(i, blocks, early=None):
-        for d in far + (0,):
-            j = up(y, d, Y)
-            total = None if early is None else PE[early, j]
-            for src, b in blocks:
-                term = product(src, b, j)
-                total = term if total is None else total + term
-            PB[i, d] = total
-            if d:
-                Copy(PB.at[i, d], RR.at[i, d], red_s.at[i, d], red_r.at[i, d], ypeer[d]).start()
+        for f in range(2):
+            for d in far:
+                j = up(y, d, Y)
+                PB[i, f, d] = products(blocks, f, j, None if early is None else PE[early, f, j])
+                Copy(PB.at[i, f, d], RR.at[i, f, d], red_s.at[i, f, d], red_r.at[i, f, d], ypeer[d]).start()
+        for f in range(2):
+            PB[i, f, 0] = products(blocks, f, y, None if early is None else PE[early, f, y])
 
     def early(slot, blocks):
-        for j in range(Y):
-            total = None
-            for src, b in blocks:
-                term = product(src, b, j)
-                total = term if total is None else total + term
-            PE[slot, j] = total
-
-    def reduce_wait(i):
-        total = PB[i, 0]
+        for f in range(2):
+            for j in range(Y):
+                PE[slot, f, j] = products(blocks, f, j)
+
+    def reduce_wait(i, f):
+        total = PB[i, f, 0]
         for d in range(1, Y):
-            arrived(RR.at[i, d], red_r.at[i, d])
-            total = total + RR[i, d]
+            arrived(RR.at[i, f, d], red_r.at[i, f, d])
+            total = total + RR[i, f, d]
         return total
 
-    def emit(s, solved, squares):
+    def emit(s):
         src = XG.at[2 * s + 1]
         for d in (4, 3, 5, 2, 6, 1, 7) if Z == 8 else range(1, Z):
             Copy(
                 src.at[up(z, d, Z), x], OB.at[s, z // 2, :, half(z)], oz_s.at[s, d], oz_r.at[s, d], zpeer[d]
             ).start()
         pltpu.make_async_copy(src.at[z, x], OB.at[s, z // 2, :, half(z)], oz_r.at[s, 0]).start()
-        part = jnp.sum(solved * solved, axis=0, keepdims=True)
-        return part if squares is None else squares + part
 
     def deliver(s):
         for d in range(Z):
@@ -306,11 +306,23 @@
         pltpu.make_async_copy(OB.at[s, x], out_ref.at[s, strip(x)], ox_r.at[s, 0]).start()
 
     def step_in(s):
-        columns = KB[s].reshape(q, w)
-        if s:
-            columns = columns - reduce_wait(2 * s - 1)
-        XG[2 * s, :, x] = columns.reshape(Z, t, w)
-        gather_start(2 * s)
+        for f in range(2):
+            columns = KB[s, pl.ds(f * H, H)].reshape(q // 2, w)
+            if s:
+                columns = columns - reduce_wait(2 * s - 1, f)
+            XG[2 * s, pl.ds(f * H, H), x] = columns.reshape(H, t, w)
+            gather_start(2 * s, f)
+
+    def step_out(s, squares):
+        for f in range(2):
+            solved = reduce_wait(2 * s, f)
+            XG[2 * s + 1, pl.ds(f * H, H), x] = solved.reshape(H, t, w)
+            if s < 3:
+                gather_start(2 * s + 1, f)
+            part = jnp.sum(solved * solved, axis=0, keepdims=True)
+            squares = part if squares is None else squares + part
+        emit(s)
+        return squares
 
     spread(0)
     columns(0)
@@ -336,10 +348,7 @@
 
     squares = None
     for s in range(3):
-        solved = reduce_wait(2 * s)
-        XG[2 * s + 1, :, x] = solved.reshape(Z, t, w)
-        gather_start(2 * s + 1)
-        squares = emit(s, solved, squares)
+        squares = step_out(s, squares)
         slot(4 * s + 6)
         if s == 0:
             finish(1)
@@ -378,9 +387,7 @@
             early(0, [(1, 1)])
         elif s == 1:
             finish(6)
-    solved = reduce_wait(6)
-    XG[7, :, x] = solved.reshape(Z, t, w)
-    squares = emit(3, solved, squares)
+    squares = step_out(3, squares)
 
     VB[0] = jnp.broadcast_to(squares, VB.shape[1:])
     for yy in range(Y):
@@ -447,14 +454,14 @@
         out_specs=(vmem, vmem),
         scratch_shapes=[
             pltpu.VMEM((10, 2, Z, X, t, wide), F32),
-            pltpu.VMEM((10, 2, X, 2 * q, wide), BF16),
+            pltpu.VMEM((10, 2, 2, X, q, wide), BF16),
             pltpu.VMEM((7, 2, X * q // 2, wide), BF16),
             pltpu.VMEM((4, X, t, wide), F32),
             pltpu.VMEM((4, Z, t, w), F32),
             pltpu.VMEM((8, Z, X, t, w), F32),
-            pltpu.VMEM((7, X, q, w), F32),
-            pltpu.VMEM((7, X, q, w), F32),
-            pltpu.VMEM((2, X, q, w), F32),
+            pltpu.VMEM((7, 2, X, q // 2, w), F32),
+            pltpu.VMEM((7, 2, X, q // 2, w), F32),
+            pltpu.VMEM((2, 2, X, q // 2, w), F32),
             pltpu.VMEM((4, X, t, wide), F32),
             pltpu.VMEM((2, 8, w), F32),
             pltpu.VMEM((X, X, 8, w), F32),
@@ -465,10 +472,10 @@
             dma((10, Z)),
             dma((10, X)),
             dma((10, X)),
-            dma((7, X)),
-            dma((7, X)),
-            dma((7, X)),
-            dma((7, X)),
+            dma((7, 2, X)),
+            dma((7, 2, X)),
+            dma((7, 2, X)),
+            dma((7, 2, X)),
             dma((2, X)),
             dma((2, X)),
             dma((2, Z)),

time: 118 us -> 118 us (level)
  no operation moved by 1% of the time
where the time goes in v3:
time: 118 us
  Pallas kernels  115 us (97%)
  local copies, waits for them, and re-layouts  2.24 us (2%)
    pallas_call x1, Pallas kernels, body(): pl.pallas_call(functools.partial(kernel, X), out_shape=(jax.ShapeDtypeStr...  115 us

profile of v3, /device:TPU:4, one launch (start us, length us, event | category | flops | bytes accessed | tf_op | source)
XLA Modules:
  0.0 117.7 jit_solution(4991280576022550452)
XLA Ops:
  0.6 114.8 %shard_map.59 = (f32[4,64,256]{2,1,0:T(8,128)}, f32[1,256]{1,0:T(1,128)}) custom-call(f32[6,64,256]{2,1,0:T(8,128)} %lower_ref.1, f32[4,64,256]{2,1,0:T(8,128)} %dinv_ref.1, f32[4,64,256]{2,1,0:T(8,128)} %kcols_ref.1, f32[1,256]{1,0:T(1,128)} %bitcast.3), custom_call_target="tpu_custom_call" | custom-call | tf_op jit(solution)/shard_map/pallas_call | solution.py:447
  115.4 0.0 copy-start
  115.4 1.7 %copy.8 = f32[4,64,256]{2,1,0:T(8,128)} copy(f32[4,64,256]{2,1,0:T(8,128)} %get-tuple-element.8) | data formatting | bytes 524288
  117.1 0.0 copy-done
  117.1 0.6 copy.9
Async XLA Ops:
  115.4 1.7 %copy-start = (f32[1,256]{1,0:T(1,128)S(1)}, f32[1,256]{1,0:T(1,128)}, u32[]{:S(2)}) copy-start(f32[1,256]{1,0:T(1,128)} %get-tuple-element.5) | copy-start | bytes 3076

commit v4 on v2

--- a/solution.py
+++ b/solution.py
@@ -187,7 +187,7 @@
             z_arrived(g, H, 2 * H - 1, upper_half)
             sib_send(g, H)
 
-    STARTS = (0, 1, 3, 5, 6, 7, 8, 9, 10, 11)
+    STARTS = (0, 1, 3, 5, 6, 8, 9, 10, 10, 12)
 
     def slot(n):
         for g, first in enumerate(STARTS):

time: 118 us -> 117 us (level)
    pallas_call x1, Pallas kernels: 115 us -> 114 us  [body(): pl.pallas_call(functools.partial(kernel, X), out_shape=(jax.ShapeDtypeStr...]
where the time goes in v4:
time: 117 us
  Pallas kernels  114 us (97%)
  local copies, waits for them, and re-layouts  2.24 us (2%)
    pallas_call x1, Pallas kernels, body(): pl.pallas_call(functools.partial(kernel, X), out_shape=(jax.ShapeDtypeStr...  114 us

profile of v4, /device:TPU:4, one launch (start us, length us, event | category | flops | bytes accessed | tf_op | source)
XLA Modules:
  0.0 116.8 jit_solution(11854105309252770502)
XLA Ops:
  0.6 113.9 %shard_map.59 = (f32[4,64,256]{2,1,0:T(8,128)}, f32[1,256]{1,0:T(1,128)}) custom-call(f32[6,64,256]{2,1,0:T(8,128)} %lower_ref.1, f32[4,64,256]{2,1,0:T(8,128)} %dinv_ref.1, f32[4,64,256]{2,1,0:T(8,128)} %kcols_ref.1, f32[1,256]{1,0:T(1,128)} %bitcast.3), custom_call_target="tpu_custom_call" | custom-call | tf_op jit(solution)/shard_map/pallas_call | solution.py:440
  114.6 0.0 copy-start
  114.6 1.7 %copy.8 = f32[4,64,256]{2,1,0:T(8,128)} copy(f32[4,64,256]{2,1,0:T(8,128)} %get-tuple-element.8) | data formatting | bytes 524288
  116.3 0.0 copy-done
  116.3 0.6 copy.9
Async XLA Ops:
  114.6 1.7 %copy-start = (f32[1,256]{1,0:T(1,128)S(1)}, f32[1,256]{1,0:T(1,128)}, u32[]{:S(2)}) copy-start(f32[1,256]{1,0:T(1,128)} %get-tuple-element.5) | copy-start | bytes 3076
